TPU v7x, 32 devices: a whole 2x2x4 slice. The times are simulated.
32 devices in a mesh: plane: 4 (over y, x), tile: 8 (over z, core).
Axes of the slice: x: 2, y: 2, z: 4, core: 2. Of those that a mesh axis runs over, the one named last changes fastest.
Arguments:
- recording: bfloat16 [4, 8, 3, 4, 256, 128], P('plane', 'tile'), may hold values from -8 to 8
- start_vectors: float32 [4, 16, 32, 128], P('plane', 'tile'), may hold values from -5 to 5
- footprints: bfloat16 [4, 1024, 256], P('plane', 'tile'), may hold values from 0.00019931793 to 0.029907227
- source_row: int32 [4, 1024, 1], P('plane', 'tile'), may hold values from 0 to 5; in each aligned block of 128 rows (0 to 127, 128 to 255, ..., all dimensions but the last counted through in order) at most 32 rows name the same one
- footprint_block: int32 [4, 1024], P('plane', 'tile'), may hold values from 0 to 3
Outputs:
- temporal_factors: float32 [4, 16, 32, 128], P('plane', 'tile')
- traces: float32 [4, 1024, 128], P('plane', 'tile')
Inputs may be any that keep to these rules, and one draw needn't show every extreme that they name: `source_row`: among the 128 sources of one device at most 32 share a value, and some value is shared by exactly 32 of them.
All inputs are finite; a program needn't handle non-finite values.
Results may differ from a plain program's by a relative error of at most 0.0069.
Values may be sent and summed in bfloat16 or wider, within the bound.
No kernel may reach another device: no remote copies, remote signals or barrier semaphores. Data moves between devices by JAX's collectives and lax.ppermute only.
A program may use at most 64 MiB of HBM per device.

v0:
```python
import jax
import jax.numpy as jnp
from jax import lax
from jax.sharding import PartitionSpec as P

ITERS = 3


def from_behind(block, axis, distance):
    devices = range(lax.axis_size(axis))
    route = [(i - distance, i) for i in devices if i - distance in devices]
    return lax.ppermute(block, axis, route)


def compress_patches(patches, start_block):
    temporal = start_block
    spatial = None
    for step_index in range(ITERS):
        projection = jnp.einsum(
            "prf,pkf->prk",
            temporal.astype(jnp.bfloat16),
            patches,
            preferred_element_type=jnp.float32,
        )
        gram_matrix = jnp.einsum(
            "prk,psk->prs", projection, projection, precision=lax.Precision.HIGHEST
        )
        cholesky_factor = jnp.linalg.cholesky(gram_matrix)
        spatial = jax.scipy.linalg.solve_triangular(cholesky_factor, projection, lower=True).astype(
            jnp.bfloat16
        )
        temporal = jnp.einsum("prk,pkf->prf", spatial, patches, preferred_element_type=jnp.float32)
    return (spatial, temporal)


def on_device(recording, start_vectors, footprints, source_row, footprint_block):
    tile_count = lax.axis_size("tile")
    own_strip = recording[0, 0]
    cell_count = own_strip.shape[0]
    patch_count = cell_count - 1
    block_pixels = own_strip.shape[2]
    frame_count = own_strip.shape[3]
    pixel_total = lax.axis_size("plane") * tile_count * cell_count * 4 * block_pixels
    frame_sum = jnp.sum(own_strip, axis=(0, 1, 2), dtype=jnp.float32)
    background = lax.psum(frame_sum, ("plane", "tile")) / pixel_total
    centered = (own_strip.astype(jnp.float32) - background).astype(jnp.bfloat16)
    lower_strip = from_behind(centered, "tile", -2)
    stacked = jnp.stack([centered, lower_strip])
    patches = jnp.stack(
        [
            stacked[:, column_index : column_index + 2].reshape(16 * block_pixels, frame_count)
            for column_index in range(patch_count)
        ]
    )
    spatial, temporal = compress_patches(patches, start_vectors[0])
    rank_width = spatial.shape[1]
    temporal_rounded = temporal.astype(jnp.bfloat16)
    source_rows = source_row[0, :, 0]
    block_value = footprint_block[0]
    footprint_rows = footprints[0]
    source_count = source_rows.shape[0]
    row_span = tile_count - 2
    capacity = max(2, (3 * source_count + 2 * row_span - 1) // (2 * row_span))
    row_match = (source_rows[:, None] == jnp.arange(tile_count)[None, :]).astype(jnp.int32)
    position = jnp.sum(jnp.cumsum(row_match, axis=0) * row_match, axis=1) - 1
    slot_upper = source_rows * capacity + position
    slot_lower = (source_rows + 2) * capacity + position
    footprint_send = jnp.zeros((tile_count * capacity, 2, block_pixels), jnp.bfloat16)
    footprint_send = (
        footprint_send.at[slot_upper, 0].set(footprint_rows).at[slot_lower, 1].set(footprint_rows)
    )
    block_send = jnp.full((tile_count * capacity, 2), -1, jnp.int32)
    block_send = block_send.at[slot_upper, 0].set(block_value).at[slot_lower, 1].set(block_value)
    footprint_send = footprint_send.reshape(tile_count, capacity, 2, block_pixels)
    block_send = block_send.reshape(tile_count, capacity, 2)
    spatial_blocks = spatial.reshape(patch_count, rank_width, 16, block_pixels)
    patch_axis = jnp.arange(patch_count)[None, None, :, None]
    block_axis = jnp.arange(8)[None, None, None, :]
    footprint_in = lax.all_to_all(footprint_send, "tile", split_axis=0, concat_axis=0, tiled=True)
    codes_in = lax.all_to_all(block_send, "tile", split_axis=0, concat_axis=0, tiled=True)
    role_terms = []
    for half_index in range(2):
        strip_offset = 1 - half_index
        block_range = spatial_blocks[:, :, strip_offset * 8 : strip_offset * 8 + 8]
        projected = jnp.einsum(
            "nkb,prgb->nkpgr",
            footprint_in[:, :, half_index],
            block_range,
            preferred_element_type=jnp.float32,
        )
        block_codes = codes_in[:, :, half_index]
        column_cell = (block_codes // 4 + 1)[:, :, None, None]
        quarter = (block_codes % 4)[:, :, None, None]
        filled = (block_codes >= 0)[:, :, None, None]
        from_left = (patch_axis == column_cell - 1) & (block_axis == quarter + 4)
        from_right = (patch_axis == column_cell) & (block_axis == quarter)
        selector = ((from_left | from_right) & filled).astype(jnp.float32)
        coefficient = jnp.sum(selector[..., None] * projected, axis=3)
        role_terms.append(
            coefficient.reshape(
                coefficient.shape[0], coefficient.shape[1], patch_count * rank_width
            )
        )
    coefficient = jnp.stack(role_terms, 2).astype(jnp.bfloat16)
    replies = lax.all_to_all(coefficient, "tile", split_axis=0, concat_axis=0, tiled=True)
    reply_rows = replies.reshape(tile_count * capacity, 2, patch_count * rank_width)
    upper_coefs = reply_rows[slot_upper, 0].reshape(source_count, patch_count, rank_width)
    lower_coefs = reply_rows[slot_lower, 1].reshape(source_count, patch_count, rank_width)
    coef_table = jnp.concatenate(
        [upper_coefs, lower_coefs, jnp.zeros((source_count, 1, rank_width), jnp.bfloat16)], 1
    )
    shard_rows = lax.all_gather(temporal_rounded, "tile", axis=0, tiled=True)
    patch_number = shard_rows.shape[0]
    patch_index = jnp.arange(patch_number)
    owner_row = patch_index // patch_count
    patch_column = patch_index % patch_count
    lookup = jnp.where(
        owner_row[None, :] == source_rows[:, None],
        patch_column[None, :],
        jnp.where(
            owner_row[None, :] == source_rows[:, None] + 2,
            patch_count + patch_column[None, :],
            2 * patch_count,
        ),
    )
    weights = jnp.take_along_axis(coef_table, lookup[:, :, None], axis=1)
    weights = weights.reshape(source_count, patch_number * rank_width)
    summed = jnp.dot(
        weights,
        shard_rows.reshape(patch_number * rank_width, frame_count),
        preferred_element_type=jnp.float32,
    )
    traces = 0.25 * summed
    return (temporal[None], traces[None])


def solution(mesh):
    placed = (
        P("plane", "tile", None, None, None, None),
        P("plane", "tile", None, None),
        P("plane", "tile", None),
        P("plane", "tile", None),
        P("plane", "tile"),
    )
    return jax.shard_map(
        on_device,
        mesh=mesh,
        in_specs=placed,
        out_specs=(P("plane", "tile", None, None), P("plane", "tile", None)),
        check_vma=False,
    )
```

profile of v0, /device:TPU:0, one launch (start us, length us, event | category | flops | bytes accessed | tf_op | source)
XLA Modules:
  0.0 174.9 jit_solution(6968167123436777132)
XLA Ops:
  0.6 1.6 convert_reduce_fusion
  2.3 42.0 %psum.7 = f32[128]{0:T(128)S(1)} all-reduce(f32[128]{0:T(128)S(1)} %convert_reduce_fusion), channel_id=1, replica_groups=mesh['plane'=4,'tile'=8] {'plane','tile'}, use_global_device_ids=true, to_apply=%region_1.0 | all-reduce | flops 128 | bytes 1024 | tf_op jit(solution)/shard_map/psum | solution.py:45
  44.5 1.3 collective-permute-start
  46.3 6.8 %scatter_fusion = s32[256,2]{0,1:T(2,128)S(1)} fusion(s32[256,2]{0,1:T(2,128)S(1)} %broadcast_in_dim.81, s32[128]{0:T(128)S(1)} %get-tuple-element.28, s32[128]{0:T(128)S(1)} %bitcast.186), kind=kCustom, calls=%fused_computation.3 | custom fusion | bytes 2560 | tf_op jit(solution)/shard_map/scatter | solution.py:73
  53.2 6.8 %scatter_fusion.1 = s32[256,2]{0,1:T(2,128)S(1)} fusion(s32[256,2]{0,1:T(2,128)S(1)} %scatter_fusion, s32[128]{0:T(128)S(1)} %get-tuple-element.29, s32[128]{0:T(128)S(1)} %bitcast.187), kind=kCustom, calls=%fused_computation.4 | custom fusion | bytes 2560 | tf_op jit(solution)/shard_map/scatter | solution.py:73
  60.7 5.7 %all-to-all-start = ((s32[8,32,2]{1,2,0:T(2,128)}), s32[8,32,2]{1,2,0:T(2,128)S(1)}, u32[]{:S(2)}, u32[]{:S(2)}) async-start(s32[8,32,2]{1,2,0:T(2,128)} %copy.50), calls=%async_computation | async-start | bytes 16384 | tf_op jit(solution)/shard_map/all_to_all | solution.py:80
  67.1 6.8 %scatter_fusion.2 = bf16[256,2,256]{2,1,0:T(2,128)(2,1)S(1)} fusion(bf16[256,2,256]{2,1,0:T(2,128)(2,1)S(1)} %broadcast_in_dim.82, s32[128]{0:T(128)S(1)} %get-tuple-element.28, bf16[128,256]{1,0:T(8,128)(2,1)S(1)} %bitcast.172), kind=kCustom, calls=%fused_computation.5 | custom fusion | bytes 197632 | tf_op jit(solution)/shard_map/scatter | solution.py:70
  73.9 6.8 %scatter_fusion.3 = bf16[256,2,256]{2,1,0:T(2,128)(2,1)S(1)} fusion(bf16[256,2,256]{2,1,0:T(2,128)(2,1)S(1)} %scatter_fusion.2, s32[128]{0:T(128)S(1)} %get-tuple-element.29, bf16[128,256]{1,0:T(8,128)(2,1)S(1)} %bitcast.173), kind=kCustom, calls=%fused_computation.6 | custom fusion | bytes 197632 | tf_op jit(solution)/shard_map/scatter | solution.py:70
  81.6 5.1 %all-to-all-start.1 = ((bf16[8,32,2,256]{3,1,2,0:T(8,128)(2,1)}), bf16[8,32,2,256]{3,1,2,0:T(8,128)(2,1)}, u32[]{:S(2)}, u32[]{:S(2)}) async-start(bf16[8,32,2,256]{3,1,2,0:T(8,128)(2,1)} %copy.52), calls=%async_computation.1 | async-start | bytes 524288 | tf_op jit(solution)/shard_map/all_to_all | solution.py:79
  89.2 1.1 fusion.41
  90.4 5.9 %custom-call.24 = f32[2,32,32]{2,1,0:T(8,128)S(1)} custom-call(f32[2,32,32]{2,1,0:T(8,128)S(1)} %fusion.24), custom_call_target="Cholesky" | custom-call | tf_op jit(solution)/shard_map/jit(cholesky)/cholesky | solution.py:28
  96.5 4.9 %custom-call.25 = f32[2,1,32,32]{2,3,1,0:T(8,128)S(1)} custom-call(f32[2,1,32,32]{3,2,1,0:T(8,128)S(1)} %select_bitcast_fusion.2), custom_call_target="InvertDiagBlocksLowerTriangular" | custom-call | tf_op jit(solution)/shard_map/jit(_solve_triangular)/vmap()/triangular_solve | solution.py:29
  101.4 1.1 convolution_convert_fusion.2
  102.5 2.7 %fusion.8 = f32[2,32,4096]{2,1,0:T(8,128)S(1)} fusion(bf16[2,32,4096]{2,1,0:T(8,128)(2,1)S(1)} %convolution_convert_fusion.2, bf16[1,4096,128]{2,1,0:T(8,128)(2,1)} %bitcast.165, bf16[1,4096,128]{2,1,0:T(8,128)(2,1)S(1)} %bitcast.161), kind=kOutput, calls=%fused_computation.29 | convolution fusion | flops 136323072 | bytes 3670016 | tf_op jit(solution)/shard_map/prf,pkf->prk/dot_general | solution.py:19
  105.2 1.1 fusion.42
  106.4 5.9 %custom-call.26 = f32[2,32,32]{2,1,0:T(8,128)S(1)} custom-call(f32[2,32,32]{2,1,0:T(8,128)S(1)} %fusion.22), custom_call_target="Cholesky" | custom-call | tf_op jit(solution)/shard_map/jit(cholesky)/cholesky | solution.py:28
  112.5 4.9 %custom-call.27 = f32[2,1,32,32]{2,3,1,0:T(8,128)S(1)} custom-call(f32[2,1,32,32]{3,2,1,0:T(8,128)S(1)} %select_bitcast_fusion.1), custom_call_target="InvertDiagBlocksLowerTriangular" | custom-call | tf_op jit(solution)/shard_map/jit(_solve_triangular)/vmap()/triangular_solve | solution.py:29
  117.4 1.1 convolution_convert_fusion.1
  118.5 2.7 %fusion.9 = f32[2,32,4096]{2,1,0:T(8,128)S(1)} fusion(bf16[2,32,4096]{2,1,0:T(8,128)(2,1)S(1)} %convolution_convert_fusion.1, bf16[1,4096,128]{2,1,0:T(8,128)(2,1)} %bitcast.166, bf16[1,4096,128]{2,1,0:T(8,128)(2,1)S(1)} %bitcast.162), kind=kOutput, calls=%fused_computation.30 | convolution fusion | flops 136323072 | bytes 3670016 | tf_op jit(solution)/shard_map/prf,pkf->prk/dot_general | solution.py:19
  121.2 1.1 fusion.43
  122.4 5.9 %custom-call.28 = f32[2,32,32]{2,1,0:T(8,128)S(1)} custom-call(f32[2,32,32]{2,1,0:T(8,128)S(1)} %fusion.20), custom_call_target="Cholesky" | custom-call | tf_op jit(solution)/shard_map/jit(cholesky)/cholesky | solution.py:28
  128.5 5.1 %custom-call.29 = f32[2,1,32,32]{2,3,1,0:T(8,128)S(1)} custom-call(f32[2,1,32,32]{3,2,1,0:T(8,128)S(1)} %select_bitcast_fusion), custom_call_target="InvertDiagBlocksLowerTriangular" | custom-call | tf_op jit(solution)/shard_map/jit(_solve_triangular)/vmap()/triangular_solve | solution.py:29
  133.6 1.0 convolution_convert_fusion
  134.8 1.7 fusion
  136.7 1.8 %fusion.1 = bf16[8,32,2,32]{1,0,3,2:T(8,128)(2,1)S(1)} fusion(f32[8,32,2,8]{1,3,0,2:T(8,128)S(1)} %copy-done.4, bf16[2,32,16,256]{3,2,1,0:T(8,128)(2,1)S(1)} %bitcast.170, bf16[8,32,2,256]{3,1,2,0:T(8,128)(2,1)} %all-to-all-done.1), kind=kOutput, calls=%fused_computation.17 | convolution fusion | flops 67354624 | bytes 491520 | tf_op jit(solution)/shard_map/nkb,prgb->nkpgr/dot_general | solution.py:85
  139.5 5.1 %all-to-all-start.2 = ((bf16[8,2,2048]{2,1,0:T(2,128)(2,1)}), bf16[8,2,2048]{2,1,0:T(2,128)(2,1)S(1)}, u32[]{:S(2)}, u32[]{:S(2)}) async-start(bf16[8,2,2048]{2,1,0:T(2,128)(2,1)} %reshape.613), calls=%async_computation.2 | async-start | bytes 131072 | tf_op jit(solution)/shard_map/all_to_all | solution.py:105
  144.6 1.1 fusion.40
  145.7 14.5 %all_gather.3 = bf16[16,32,128]{2,1,0:T(8,128)(2,1)S(1)} all-gather(bf16[2,32,128]{2,1,0:T(8,128)(2,1)S(1)} %get-tuple-element.26), channel_id=1, replica_groups=mesh['plane'=4,'tile'=8] {'tile'}, dimensions={0}, use_global_device_ids=true | all-gather | bytes 147456 | tf_op jit(solution)/shard_map/all_gather | solution.py:112
  160.4 1.0 gather_fusion.1
  161.6 1.0 gather_fusion
  163.0 10.6 %gather_fusion.2 = bf16[2048,32]{1,0:T(8,128)(2,1)S(1)} fusion(bf16[128,5,32]{2,0,1:T(8,128)(2,1)S(1)} %copy.61, s32[2048]{0:T(1024)S(1)} %reshape.577), kind=kCustom, calls=%fused_computation.2 | custom fusion | bytes 278528 | tf_op jit(solution)/shard_map/jit(take_along_axis)/gather | solution.py:126
  174.0 0.9 fusion.7
  (86 shorter events, 8.4 us)
Async XLA Ops:
  0.6 43.7 %copy-start = (bf16[1,1,3,4,256,128]{5,4,3,2,1,0:T(8,128)(2,1)S(1)}, bf16[1,1,3,4,256,128]{5,4,3,2,1,0:T(8,128)(2,1)}, u32[]{:S(2)}) copy-start(bf16[1,1,3,4,256,128]{5,4,3,2,1,0:T(8,128)(2,1)} %param.8) | copy-start | bytes 2359300
  0.6 45.2 %copy-start.5 = (s32[1,128,1]{1,2,0:T(1,128)S(1)}, s32[1,128,1]{1,2,0:T(1,128)}, u32[]{:S(2)}) copy-start(s32[1,128,1]{1,2,0:T(1,128)} %param.11) | copy-start | bytes 1540
  2.3 44.0 %copy-start.6 = (s32[1,128]{1,0:T(1,128)S(1)}, s32[1,128]{1,0:T(1,128)}, u32[]{:S(2)}) copy-start(s32[1,128]{1,0:T(1,128)} %param.12) | copy-start | bytes 1540
  44.5 43.1 %collective-permute-start = (bf16[3,4,256,128]{3,2,1,0:T(8,128)(2,1)S(1)}, bf16[3,4,256,128]{3,2,1,0:T(8,128)(2,1)S(1)}, u32[]{:S(2)}, u32[]{:S(2)}) collective-permute-start(bf16[3,4,256,128]{3,2,1,0:T(8,128)(2,1)S(1)} %fusion.5), channel_id=1, source_target_pairs={{2,0},{3,1},{4,2},{5,3},{6,4},{7,5},{10,8},{11,9},{12,10},{13,11},... | collective-permute-start | bytes 2359304 | tf_op jit(solution)/shard_map/ppermute | solution.py:12
  60.0 7.0 %copy-start.3 = (bf16[1,128,256]{2,1,0:T(8,128)(2,1)S(1)}, bf16[1,128,256]{2,1,0:T(8,128)(2,1)}, u32[]{:S(2)}) copy-start(bf16[1,128,256]{2,1,0:T(8,128)(2,1)} %param.10) | copy-start | bytes 196612
  60.7 20.9 %all-to-all-start = ((s32[8,32,2]{1,2,0:T(2,128)}), s32[8,32,2]{1,2,0:T(2,128)S(1)}, u32[]{:S(2)}, u32[]{:S(2)}) async-start(s32[8,32,2]{1,2,0:T(2,128)} %copy.50), calls=%async_computation | async-start | bytes 16384 | tf_op jit(solution)/shard_map/all_to_all | solution.py:80
  81.6 53.1 %all-to-all-start.1 = ((bf16[8,32,2,256]{3,1,2,0:T(8,128)(2,1)}), bf16[8,32,2,256]{3,1,2,0:T(8,128)(2,1)}, u32[]{:S(2)}, u32[]{:S(2)}) async-start(bf16[8,32,2,256]{3,1,2,0:T(8,128)(2,1)} %copy.52), calls=%async_computation.1 | async-start | bytes 524288 | tf_op jit(solution)/shard_map/all_to_all | solution.py:79
  87.6 0.8 copy-start.7
  87.8 1.4 copy-start.1
  134.8 1.9 %copy-start.4 = (f32[8,32,2,8]{1,3,0,2:T(8,128)S(1)}, f32[8,32,2,8]{1,3,0,2:T(8,128)}, u32[]{:S(2)}) copy-start(f32[8,32,2,8]{1,3,0,2:T(8,128)} %and_convert_fusion.1) | copy-start | bytes 49156
  136.7 7.9 %copy-start.2 = (bf16[2,2,4,256,128]{4,3,2,1,0:T(8,128)(2,1)S(1)}, bf16[2,2,4,256,128]{4,3,2,1,0:T(8,128)(2,1)}, u32[]{:S(2)}) copy-start(bf16[2,2,4,256,128]{4,3,2,1,0:T(8,128)(2,1)} %copy-done.1) | copy-start | bytes 3145732
  139.5 20.7 %all-to-all-start.2 = ((bf16[8,2,2048]{2,1,0:T(2,128)(2,1)}), bf16[8,2,2048]{2,1,0:T(2,128)(2,1)S(1)}, u32[]{:S(2)}, u32[]{:S(2)}) async-start(bf16[8,2,2048]{2,1,0:T(2,128)(2,1)} %reshape.613), calls=%async_computation.2 | async-start | bytes 131072 | tf_op jit(solution)/shard_map/all_to_all | solution.py:105
where the time goes:
time: 175 us
  blocking collectives  56.5 us (32%)
  local copies, waits for them, and re-layouts  44.8 us (26%)
  other arithmetic  37 us (21%)
  matrix products  18.2 us (10%)
  starting transfers between devices  17.2 us (10%)
    psum x1, blocking collectives, on_device(): background = lax.psum(frame_sum, ('plane', 'tile')) / pixel_total  42 us
    another operation x10, other arithmetic, compress_patches(): cholesky_factor = jnp.linalg.cholesky(gram_matrix)  18.1 us
    another operation x7, other arithmetic, compress_patches(): jax.scipy.linalg.solve_triangular(cholesky_factor, projection, lower=True)  15.2 us
    all_gather x1, blocking collectives, on_device(): shard_rows = lax.all_gather(temporal_rounded, 'tile', axis=0, tiled=True)  14.5 us
    scatter x2, local copies, waits for them, and re-layouts, on_device(): block_send.at[slot_upper, 0].set(block_value).at[slot_lower, 1]  13.7 us
    scatter x2, local copies, waits for them, and re-layouts, on_device(): footprint_send.at[slot_upper, 0].set(footprint_rows).at[slot_lower, 1]  13.6 us
    gather x3, local copies, waits for them, and re-layouts, on_device(): weights = jnp.take_along_axis(coef_table, lookup[:, :, None], axis=1)  11.1 us
    dot_general x3, matrix products, compress_patches(): jnp.einsum('prf,pkf->prk', temporal.astype(jnp.bfloat16), patches, prefer...  6.26 us
  transfers between devices with their start and end apart: 4, of which 0 were waited for; matrix products, arithmetic and copies ran while one was open for 45% of the time, Pallas kernels for 0%

commit v1 on v0

--- a/solution.py
+++ b/solution.py
@@ -42,7 +42,7 @@
     frame_count = own_strip.shape[3]
     pixel_total = lax.axis_size("plane") * tile_count * cell_count * 4 * block_pixels
     frame_sum = jnp.sum(own_strip, axis=(0, 1, 2), dtype=jnp.float32)
-    background = lax.psum(frame_sum, ("plane", "tile")) / pixel_total
+    background = jnp.sum(lax.all_gather(frame_sum, ("plane", "tile")), axis=0) / pixel_total
     centered = (own_strip.astype(jnp.float32) - background).astype(jnp.bfloat16)
     lower_strip = from_behind(centered, "tile", -2)
     stacked = jnp.stack([centered, lower_strip])

time: 175 us -> 175 us (level)
  starting transfers between devices: 17.2 us -> 15.4 us
    all_gather x0 -> x1, blocking collectives: none -> 43.1 us  [on_device(): lax.all_gather(frame_sum, ('plane', 'tile'))]
    psum x1 -> x0, blocking collectives: 42 us -> none  [on_device(): background = lax.psum(frame_sum, ('plane', 'tile')) / pixel_total]
    all_to_all x1, starting transfers between devices: 5.73 us -> 3.92 us  [on_device(): lax.all_to_all(block_send, 'tile', split_axis=0, concat_axis=0, tiled=True)]
where the time goes in v1:
time: 175 us; the launch traced here: 174 us
  blocking collectives  57.6 us (33%)
  local copies, waits for them, and re-layouts  44.8 us (26%)
  other arithmetic  37.1 us (21%)
  matrix products  18.2 us (10%)
  starting transfers between devices  15.4 us (9%)
    all_gather x1, blocking collectives, on_device(): lax.all_gather(frame_sum, ('plane', 'tile'))  43.1 us
    another operation x10, other arithmetic, compress_patches(): cholesky_factor = jnp.linalg.cholesky(gram_matrix)  18.1 us
    another operation x7, other arithmetic, compress_patches(): jax.scipy.linalg.solve_triangular(cholesky_factor, projection, lower=True)  15.2 us
    all_gather x1, blocking collectives, on_device(): shard_rows = lax.all_gather(temporal_rounded, 'tile', axis=0, tiled=True)  14.5 us
    scatter x2, local copies, waits for them, and re-layouts, on_device(): block_send.at[slot_upper, 0].set(block_value).at[slot_lower, 1]  13.7 us
    scatter x2, local copies, waits for them, and re-layouts, on_device(): footprint_send.at[slot_upper, 0].set(footprint_rows).at[slot_lower, 1]  13.6 us
    gather x3, local copies, waits for them, and re-layouts, on_device(): weights = jnp.take_along_axis(coef_table, lookup[:, :, None], axis=1)  11.1 us
    dot_general x3, matrix products, compress_patches(): jnp.einsum('prf,pkf->prk', temporal.astype(jnp.bfloat16), patches, prefer...  6.26 us
  transfers between devices with their start and end apart: 4, of which 0 were waited for; matrix products, arithmetic and copies ran while one was open for 45% of the time, Pallas kernels for 0%

profile of v1, /device:TPU:0, one launch (start us, length us, event | category | flops | bytes accessed | tf_op | source)
XLA Modules:
  0.0 174.1 jit_solution(17476929599759178963)
XLA Ops:
  0.6 1.6 convert_reduce_fusion
  2.3 43.1 %all-gather.1 = f32[32,1,128]{2,1,0:T(1,128)S(1)} all-gather(f32[1,1,128]{2,1,0:T(1,128)S(1)} %bitcast.189), channel_id=2, replica_groups=mesh['plane'=4,'tile'=8] {'plane','tile'}, dimensions={0}, use_global_device_ids=true | all-gather | bytes 16896 | tf_op jit(solution)/shard_map/all_gather | solution.py:45
  45.6 1.3 collective-permute-start
  47.4 6.8 %scatter_fusion = s32[256,2]{0,1:T(2,128)S(1)} fusion(s32[256,2]{0,1:T(2,128)S(1)} %broadcast_in_dim.81, s32[128]{0:T(128)S(1)} %get-tuple-element.28, s32[128]{0:T(128)S(1)} %bitcast.187), kind=kCustom, calls=%fused_computation.3 | custom fusion | bytes 2560 | tf_op jit(solution)/shard_map/scatter | solution.py:73
  54.3 6.8 %scatter_fusion.1 = s32[256,2]{0,1:T(2,128)S(1)} fusion(s32[256,2]{0,1:T(2,128)S(1)} %scatter_fusion, s32[128]{0:T(128)S(1)} %get-tuple-element.29, s32[128]{0:T(128)S(1)} %bitcast.188), kind=kCustom, calls=%fused_computation.4 | custom fusion | bytes 2560 | tf_op jit(solution)/shard_map/scatter | solution.py:73
  61.8 3.9 %all-to-all-start = ((s32[8,32,2]{1,2,0:T(2,128)}), s32[8,32,2]{1,2,0:T(2,128)S(1)}, u32[]{:S(2)}, u32[]{:S(2)}) async-start(s32[8,32,2]{1,2,0:T(2,128)} %copy.50), calls=%async_computation | async-start | bytes 16384 | tf_op jit(solution)/shard_map/all_to_all | solution.py:80
  66.4 6.8 %scatter_fusion.2 = bf16[256,2,256]{2,1,0:T(2,128)(2,1)S(1)} fusion(bf16[256,2,256]{2,1,0:T(2,128)(2,1)S(1)} %broadcast_in_dim.82, s32[128]{0:T(128)S(1)} %get-tuple-element.28, bf16[128,256]{1,0:T(8,128)(2,1)S(1)} %bitcast.173), kind=kCustom, calls=%fused_computation.5 | custom fusion | bytes 197632 | tf_op jit(solution)/shard_map/scatter | solution.py:70
  73.2 6.8 %scatter_fusion.3 = bf16[256,2,256]{2,1,0:T(2,128)(2,1)S(1)} fusion(bf16[256,2,256]{2,1,0:T(2,128)(2,1)S(1)} %scatter_fusion.2, s32[128]{0:T(128)S(1)} %get-tuple-element.29, bf16[128,256]{1,0:T(8,128)(2,1)S(1)} %bitcast.174), kind=kCustom, calls=%fused_computation.6 | custom fusion | bytes 197632 | tf_op jit(solution)/shard_map/scatter | solution.py:70
  80.9 5.1 %all-to-all-start.1 = ((bf16[8,32,2,256]{3,1,2,0:T(8,128)(2,1)}), bf16[8,32,2,256]{3,1,2,0:T(8,128)(2,1)}, u32[]{:S(2)}, u32[]{:S(2)}) async-start(bf16[8,32,2,256]{3,1,2,0:T(8,128)(2,1)} %copy.52), calls=%async_computation.1 | async-start | bytes 524288 | tf_op jit(solution)/shard_map/all_to_all | solution.py:79
  88.5 1.1 fusion.41
  89.7 5.9 %custom-call.24 = f32[2,32,32]{2,1,0:T(8,128)S(1)} custom-call(f32[2,32,32]{2,1,0:T(8,128)S(1)} %fusion.24), custom_call_target="Cholesky" | custom-call | tf_op jit(solution)/shard_map/jit(cholesky)/cholesky | solution.py:28
  95.8 4.9 %custom-call.25 = f32[2,1,32,32]{2,3,1,0:T(8,128)S(1)} custom-call(f32[2,1,32,32]{3,2,1,0:T(8,128)S(1)} %select_bitcast_fusion.2), custom_call_target="InvertDiagBlocksLowerTriangular" | custom-call | tf_op jit(solution)/shard_map/jit(_solve_triangular)/vmap()/triangular_solve | solution.py:29
  100.7 1.1 convolution_convert_fusion.2
  101.8 2.7 %fusion.8 = f32[2,32,4096]{2,1,0:T(8,128)S(1)} fusion(bf16[2,32,4096]{2,1,0:T(8,128)(2,1)S(1)} %convolution_convert_fusion.2, bf16[1,4096,128]{2,1,0:T(8,128)(2,1)} %bitcast.166, bf16[1,4096,128]{2,1,0:T(8,128)(2,1)S(1)} %bitcast.162), kind=kOutput, calls=%fused_computation.29 | convolution fusion | flops 136323072 | bytes 3670016 | tf_op jit(solution)/shard_map/prf,pkf->prk/dot_general | solution.py:19
  104.5 1.1 fusion.42
  105.7 5.9 %custom-call.26 = f32[2,32,32]{2,1,0:T(8,128)S(1)} custom-call(f32[2,32,32]{2,1,0:T(8,128)S(1)} %fusion.22), custom_call_target="Cholesky" | custom-call | tf_op jit(solution)/shard_map/jit(cholesky)/cholesky | solution.py:28
  111.8 4.9 %custom-call.27 = f32[2,1,32,32]{2,3,1,0:T(8,128)S(1)} custom-call(f32[2,1,32,32]{3,2,1,0:T(8,128)S(1)} %select_bitcast_fusion.1), custom_call_target="InvertDiagBlocksLowerTriangular" | custom-call | tf_op jit(solution)/shard_map/jit(_solve_triangular)/vmap()/triangular_solve | solution.py:29
  116.7 1.1 convolution_convert_fusion.1
  117.8 2.7 %fusion.9 = f32[2,32,4096]{2,1,0:T(8,128)S(1)} fusion(bf16[2,32,4096]{2,1,0:T(8,128)(2,1)S(1)} %convolution_convert_fusion.1, bf16[1,4096,128]{2,1,0:T(8,128)(2,1)} %bitcast.167, bf16[1,4096,128]{2,1,0:T(8,128)(2,1)S(1)} %bitcast.163), kind=kOutput, calls=%fused_computation.30 | convolution fusion | flops 136323072 | bytes 3670016 | tf_op jit(solution)/shard_map/prf,pkf->prk/dot_general | solution.py:19
  120.5 1.1 fusion.43
  121.7 5.9 %custom-call.28 = f32[2,32,32]{2,1,0:T(8,128)S(1)} custom-call(f32[2,32,32]{2,1,0:T(8,128)S(1)} %fusion.20), custom_call_target="Cholesky" | custom-call | tf_op jit(solution)/shard_map/jit(cholesky)/cholesky | solution.py:28
  127.8 5.1 %custom-call.29 = f32[2,1,32,32]{2,3,1,0:T(8,128)S(1)} custom-call(f32[2,1,32,32]{3,2,1,0:T(8,128)S(1)} %select_bitcast_fusion), custom_call_target="InvertDiagBlocksLowerTriangular" | custom-call | tf_op jit(solution)/shard_map/jit(_solve_triangular)/vmap()/triangular_solve | solution.py:29
  132.9 1.0 convolution_convert_fusion
  134.1 1.7 fusion
  136.0 1.8 %fusion.1 = bf16[8,32,2,32]{1,0,3,2:T(8,128)(2,1)S(1)} fusion(f32[8,32,2,8]{1,3,0,2:T(8,128)S(1)} %copy-done.4, bf16[2,32,16,256]{3,2,1,0:T(8,128)(2,1)S(1)} %bitcast.171, bf16[8,32,2,256]{3,1,2,0:T(8,128)(2,1)} %all-to-all-done.1), kind=kOutput, calls=%fused_computation.17 | convolution fusion | flops 67354624 | bytes 491520 | tf_op jit(solution)/shard_map/nkb,prgb->nkpgr/dot_general | solution.py:85
  138.8 5.1 %all-to-all-start.2 = ((bf16[8,2,2048]{2,1,0:T(2,128)(2,1)}), bf16[8,2,2048]{2,1,0:T(2,128)(2,1)S(1)}, u32[]{:S(2)}, u32[]{:S(2)}) async-start(bf16[8,2,2048]{2,1,0:T(2,128)(2,1)} %reshape.619), calls=%async_computation.2 | async-start | bytes 131072 | tf_op jit(solution)/shard_map/all_to_all | solution.py:105
  143.9 1.1 fusion.40
  145.0 14.5 %all_gather.11 = bf16[16,32,128]{2,1,0:T(8,128)(2,1)S(1)} all-gather(bf16[2,32,128]{2,1,0:T(8,128)(2,1)S(1)} %get-tuple-element.26), channel_id=1, replica_groups=mesh['plane'=4,'tile'=8] {'tile'}, dimensions={0}, use_global_device_ids=true | all-gather | bytes 147456 | tf_op jit(solution)/shard_map/all_gather | solution.py:112
  159.7 1.0 gather_fusion.1
  160.8 1.0 gather_fusion
  162.2 10.6 %gather_fusion.2 = bf16[2048,32]{1,0:T(8,128)(2,1)S(1)} fusion(bf16[128,5,32]{2,0,1:T(8,128)(2,1)S(1)} %copy.61, s32[2048]{0:T(1024)S(1)} %reshape.579), kind=kCustom, calls=%fused_computation.2 | custom fusion | bytes 278528 | tf_op jit(solution)/shard_map/jit(take_along_axis)/gather | solution.py:126
  173.3 0.9 fusion.7
  (87 shorter events, 8.5 us)
Async XLA Ops:
  0.6 44.8 %copy-start = (bf16[1,1,3,4,256,128]{5,4,3,2,1,0:T(8,128)(2,1)S(1)}, bf16[1,1,3,4,256,128]{5,4,3,2,1,0:T(8,128)(2,1)}, u32[]{:S(2)}) copy-start(bf16[1,1,3,4,256,128]{5,4,3,2,1,0:T(8,128)(2,1)} %param.8) | copy-start | bytes 2359300
  0.6 46.3 %copy-start.5 = (s32[1,128,1]{1,2,0:T(1,128)S(1)}, s32[1,128,1]{1,2,0:T(1,128)}, u32[]{:S(2)}) copy-start(s32[1,128,1]{1,2,0:T(1,128)} %param.11) | copy-start | bytes 1540
  2.3 45.1 %copy-start.6 = (s32[1,128]{1,0:T(1,128)S(1)}, s32[1,128]{1,0:T(1,128)}, u32[]{:S(2)}) copy-start(s32[1,128]{1,0:T(1,128)} %param.12) | copy-start | bytes 1540
  45.6 41.3 %collective-permute-start = (bf16[3,4,256,128]{3,2,1,0:T(8,128)(2,1)S(1)}, bf16[3,4,256,128]{3,2,1,0:T(8,128)(2,1)S(1)}, u32[]{:S(2)}, u32[]{:S(2)}) collective-permute-start(bf16[3,4,256,128]{3,2,1,0:T(8,128)(2,1)S(1)} %fusion.5), channel_id=1, source_target_pairs={{2,0},{3,1},{4,2},{5,3},{6,4},{7,5},{10,8},{11,9},{12,10},{13,11},... | collective-permute-start | bytes 2359304 | tf_op jit(solution)/shard_map/ppermute | solution.py:12
  61.1 5.2 %copy-start.3 = (bf16[1,128,256]{2,1,0:T(8,128)(2,1)S(1)}, bf16[1,128,256]{2,1,0:T(8,128)(2,1)}, u32[]{:S(2)}) copy-start(bf16[1,128,256]{2,1,0:T(8,128)(2,1)} %param.10) | copy-start | bytes 196612
  61.8 19.1 %all-to-all-start = ((s32[8,32,2]{1,2,0:T(2,128)}), s32[8,32,2]{1,2,0:T(2,128)S(1)}, u32[]{:S(2)}, u32[]{:S(2)}) async-start(s32[8,32,2]{1,2,0:T(2,128)} %copy.50), calls=%async_computation | async-start | bytes 16384 | tf_op jit(solution)/shard_map/all_to_all | solution.py:80
  80.9 53.1 %all-to-all-start.1 = ((bf16[8,32,2,256]{3,1,2,0:T(8,128)(2,1)}), bf16[8,32,2,256]{3,1,2,0:T(8,128)(2,1)}, u32[]{:S(2)}, u32[]{:S(2)}) async-start(bf16[8,32,2,256]{3,1,2,0:T(8,128)(2,1)} %copy.52), calls=%async_computation.1 | async-start | bytes 524288 | tf_op jit(solution)/shard_map/all_to_all | solution.py:79
  86.9 0.8 copy-start.7
  87.1 1.4 copy-start.1
  134.0 1.9 %copy-start.4 = (f32[8,32,2,8]{1,3,0,2:T(8,128)S(1)}, f32[8,32,2,8]{1,3,0,2:T(8,128)}, u32[]{:S(2)}) copy-start(f32[8,32,2,8]{1,3,0,2:T(8,128)} %and_convert_fusion.1) | copy-start | bytes 49156
  136.0 7.9 %copy-start.2 = (bf16[2,2,4,256,128]{4,3,2,1,0:T(8,128)(2,1)S(1)}, bf16[2,2,4,256,128]{4,3,2,1,0:T(8,128)(2,1)}, u32[]{:S(2)}) copy-start(bf16[2,2,4,256,128]{4,3,2,1,0:T(8,128)(2,1)} %copy-done.1) | copy-start | bytes 3145732
  138.8 20.7 %all-to-all-start.2 = ((bf16[8,2,2048]{2,1,0:T(2,128)(2,1)}), bf16[8,2,2048]{2,1,0:T(2,128)(2,1)S(1)}, u32[]{:S(2)}, u32[]{:S(2)}) async-start(bf16[8,2,2048]{2,1,0:T(2,128)(2,1)} %reshape.619), calls=%async_computation.2 | async-start | bytes 131072 | tf_op jit(solution)/shard_map/all_to_all | solution.py:105
